TPU v7x, 128 devices: a whole 4x4x4 slice. The times are simulated.
128 devices in a mesh: fx: 16 (over x, z), fy: 8 (over y, core).
Axes of the slice: x: 4, y: 4, z: 4, core: 2. Of those that a mesh axis runs over, the one named last changes fastest.
Arguments:
- fluid_state: float32 [5, 8, 2048, 1024], P(None, None, 'fx', 'fy'), may hold values from -0.3 to 2.8, as said below
- surface_points: float32 [16384, 3, 128], P(('fx', 'fy')), may hold values from 0 to 1
- surface_normals: float32 [16384, 3, 128], P(('fx', 'fy')), may hold values from -1 to 1
- owner_ids: int32 [16384, 1], P(('fx', 'fy')), may hold values from 0 to 127; in each aligned block of 128 rows (0 to 127, 128 to 255, ...) at most 2 rows name the same one
- support_ids: int32 [16384, 2], P(('fx', 'fy')), may hold values from 0 to 7
- struct_points: float32 [1024, 3, 128], P(('fx', 'fy')), may hold values from 0 to 1
- couplings: float32 [1024, 4, 128, 128], P(('fx', 'fy')), may hold values from 0.5 to 1
- coupling_pattern: int32 [1024, 4], P(('fx', 'fy')), may hold values from 0 to 7, as said below
- stiff_diagonal: float32 [1024, 128], P(('fx', 'fy')), may hold values from 1.05 to 1.6
- struct_load: float32 [1024, 3, 128], P(('fx', 'fy')), may hold values from -6 to 6
- predicted: float32 [1024, 3, 128], P(('fx', 'fy')), may hold values from -3 to 3
- hist_residual: float32 [8, 1024, 3, 128], P(None, ('fx', 'fy')), may hold values from -0.03 to 0.03
- hist_response: float32 [8, 1024, 3, 128], P(None, ('fx', 'fy')), may hold values from -6 to 6
Outputs:
- new_state: float32 [5, 8, 2048, 1024], P(None, None, 'fx', 'fy')
- next_estimate: float32 [1024, 3, 128], P(('fx', 'fy'))
- coupling_residual: float32 [1024, 3, 128], P(('fx', 'fy'))
Inputs may be any that keep to these rules, and one draw needn't show every extreme that they name: `fluid_state`: component 0 (density) lies in [0.8, 1.2], components 1 to 3 (momenta) in [-0.3, 0.3], component 4 (total energy) in [2.2, 2.8]. `owner_ids`: among the 128 surface blocks of one device (aligned blocks of rows), no owner is named by more than 2 of them. `support_ids`: local block numbers on the owner. For each device's 8 structure blocks and each column k, the entries coupling_pattern[., k] are a permutation of 0 to 7.
All inputs are finite; a program needn't handle non-finite values.
Results may differ from a plain program's by a relative error of at most 0.0003.
Values sent between devices are 32-bit elements; how exact they have to be, the bound alone decides.
No kernel may reach another device: no remote copies, remote signals or barrier semaphores. Data moves between devices by JAX's collectives and lax.ppermute only.
A program may use at most 192 MiB of HBM per device.

v0:
```python
import math
import jax
import jax.numpy as jnp
from jax import lax
from jax.sharding import PartitionSpec as P

CG_ITERS = 2
COUPLE = 2
TOP_PRECISION = lax.Precision.HIGHEST
STEP_RATIO = 0.12
WALL_SPEED = 0.5
WALL_GAIN = 0.5
LOAD_SCALE = 4.0
PRESSURE_REF = 0.98
RADIUS = 1.0


def with_halo(cells, sides, width):
    for axis, dim in sides:
        count = lax.axis_size(axis)
        head = lax.slice_in_dim(cells, 0, width, axis=dim)
        tail = lax.slice_in_dim(cells, cells.shape[dim] - width, cells.shape[dim], axis=dim)
        cells = jnp.concatenate(
            [
                lax.ppermute(tail, axis, [(i, (i + 1) % count) for i in range(count)]),
                cells,
                lax.ppermute(head, axis, [((i + 1) % count, i) for i in range(count)]),
            ],
            axis=dim,
        )
    return cells


def state_pressure(state):
    return 0.4 * (
        state[4]
        - 0.5 * (state[1] * state[1] + state[2] * state[2] + state[3] * state[3]) / state[0]
    )


def face_terms(state, momentum):
    density = state[0]
    velocity = state[momentum] / density
    pressure = state_pressure(state)
    flux = state * velocity
    flux = flux.at[momentum].add(pressure)
    flux = flux.at[4].add(pressure * velocity)
    speed = jnp.abs(velocity) + jnp.sqrt(1.4 * pressure / density)
    return (flux, speed)


def rusanov(left, right, left_flux, right_flux, left_speed, right_speed):
    return 0.5 * (left_flux + right_flux) - 0.5 * jnp.maximum(left_speed, right_speed) * (
        right - left
    )


def vertical_terms(state, wall):
    bottom = state[:, 0]
    ghost = bottom.at[3].set(2.0 * bottom[0] * wall - bottom[3])
    column = jnp.concatenate([ghost[:, None], state, state[:, -1:]], axis=1)
    flux, speed = face_terms(column, 3)
    faces = rusanov(column[:, :-1], column[:, 1:], flux[:, :-1], flux[:, 1:], speed[:-1], speed[1:])
    return faces[:, 1:] - faces[:, :-1]


def horizontal_terms(state):
    extended = with_halo(state, (("fx", 2), ("fy", 3)), 1)
    strip = extended[:, :, :, 1:-1]
    flux, speed = face_terms(strip, 1)
    faces = rusanov(
        strip[:, :, :-1],
        strip[:, :, 1:],
        flux[:, :, :-1],
        flux[:, :, 1:],
        speed[:, :-1],
        speed[:, 1:],
    )
    total = faces[:, :, 1:] - faces[:, :, :-1]
    strip = extended[:, :, 1:-1, :]
    flux, speed = face_terms(strip, 2)
    faces = rusanov(
        strip[:, :, :, :-1],
        strip[:, :, :, 1:],
        flux[:, :, :, :-1],
        flux[:, :, :, 1:],
        speed[:, :, :-1],
        speed[:, :, 1:],
    )
    return total + (faces[:, :, :, 1:] - faces[:, :, :, :-1])


def kernel_block(fluid_points, struct_nodes):
    squared = jnp.zeros((), jnp.float32)
    for axis in range(3):
        offset = fluid_points[..., axis, :, None] - struct_nodes[..., axis, None, :]
        squared = squared + offset * offset
    ratio = jnp.sqrt(squared) / RADIUS
    reach = jnp.maximum(1.0 - ratio, 0.0)
    return reach * reach * reach * reach * (4.0 * ratio + 1.0)


def owner_kernels(places, support, struct_points):
    rows = places.shape[0]
    points = places.shape[-1]
    spread = support.shape[1]
    group = math.gcd(rows, 16)

    def one_group(inputs):
        where, which = inputs
        return kernel_block(where[:, None], struct_points[which])

    kernels = lax.map(
        one_group, (places.reshape(-1, group, 3, points), support.reshape(-1, group, spread))
    )
    return kernels.reshape(rows, spread, points, points)


def owner_motion(kernels, support, field_values):
    return jnp.einsum("gkij,gkcj->gci", kernels, field_values[support], precision=TOP_PRECISION)


def owner_loads(kernels, support, blocks, traction):
    flux_terms = jnp.einsum("gkij,gci->gkcj", kernels, traction, precision=TOP_PRECISION)
    selector = (support[:, :, None] == jnp.arange(blocks, dtype=jnp.int32)[None, None, :]).astype(
        jnp.float32
    )
    return jnp.einsum("rke,rkcj->ecj", selector, flux_terms, precision=TOP_PRECISION)


def route_coords(geometry, support):
    moved_geometry, moved_support = (
        lax.all_to_all(geometry, ("fx", "fy"), split_axis=0, concat_axis=0, tiled=True),
        lax.all_to_all(support, ("fx", "fy"), split_axis=0, concat_axis=0, tiled=True),
    )
    return (moved_geometry, moved_support)


def route_field(values):
    return lax.all_to_all(values, ("fx", "fy"), split_axis=0, concat_axis=0, tiled=True)


def global_sums(values):
    return lax.psum(values, ("fx", "fy"))


def stiffness(field_values, couplings, sparsity_layout, selector, diagonal):
    blocks = field_values.shape[0]
    scale = 1.0 / (2.0 * couplings.shape[1] * couplings.shape[2])
    flux_terms = jnp.einsum("aosq,avs->aovq", couplings, field_values, precision=TOP_PRECISION)
    shipped = jnp.einsum("bke,bkdj->edj", selector, flux_terms, precision=TOP_PRECISION)
    stacked = jnp.concatenate([shipped, field_values], axis=0)
    extended = with_halo(stacked, ((("fx", "fy"), 0),), blocks)
    prior_iterate = extended[:blocks]
    later = extended[-blocks:]
    forward_pass = jnp.einsum(
        "hzwm,hzlm->hlw", couplings, prior_iterate[sparsity_layout], precision=TOP_PRECISION
    )
    return diagonal[:, None, :] * field_values - scale * (forward_pass + later)


def conjugate(start, rhs, operate):
    residual = rhs - operate(start)
    solution = start
    direction = residual
    norm_now = global_sums(jnp.stack([jnp.sum(residual * residual)]))[0]
    for count in range(CG_ITERS):
        image = operate(direction)
        alpha = norm_now / global_sums(jnp.stack([jnp.sum(direction * image)]))[0]
        solution = solution + alpha * direction
        residual = residual - alpha * image
        if count + 1 < CG_ITERS:
            norm_next = global_sums(jnp.stack([jnp.sum(residual * residual)]))[0]
            direction = residual + norm_next / norm_now * direction
            norm_now = norm_next
    return solution


def newton_update(response, gram, projected, responses):
    lower = jnp.linalg.cholesky(gram)
    middle = lax.linalg.triangular_solve(lower, projected[:, None], left_side=True, lower=True)
    weights = lax.linalg.triangular_solve(
        lower, middle, left_side=True, lower=True, transpose_a=True
    )[:, 0]
    return response - jnp.einsum("h,hbdp->bdp", weights, responses, precision=TOP_PRECISION)


def on_device(
    fluid_state,
    surface_points,
    surface_normals,
    owner_ids,
    support_ids,
    struct_points,
    couplings,
    coupling_pattern,
    stiff_diagonal,
    struct_load,
    predicted,
    hist_residual,
    hist_response,
):
    rows_fx = lax.axis_size("fx")
    rows_fy = lax.axis_size("fy")
    devices = rows_fx * rows_fy
    surface_count = owner_ids.shape[0]
    capacity = max(2, 2 * surface_count // devices)
    owners = owner_ids[:, 0]
    chosen = (owners[:, None] == jnp.arange(devices, dtype=jnp.int32)[None, :]).astype(jnp.int32)
    slots = owners * capacity + jnp.sum((jnp.cumsum(chosen, axis=0) - chosen) * chosen, axis=1)
    width = devices * capacity

    def pack(values):
        return jnp.zeros((width,) + values.shape[1:], values.dtype).at[slots].set(values)

    owner_geometry, owner_support = route_coords(pack(surface_points), pack(support_ids))
    kernels = owner_kernels(owner_geometry, owner_support, struct_points)
    blocks = couplings.shape[0]
    selector = (
        coupling_pattern[:, :, None] == jnp.arange(blocks, dtype=jnp.int32)[None, None, :]
    ).astype(jnp.float32)

    def operate(field_values):
        return stiffness(field_values, couplings, coupling_pattern, selector, stiff_diagonal)

    horizontal = horizontal_terms(fluid_state)
    estimate = predicted
    differences = hist_residual
    responses = hist_response
    last_residual = predicted
    last_response = predicted
    new_state = fluid_state
    residual = predicted
    for count in range(COUPLE):
        motion_slots = owner_motion(kernels, owner_support, estimate)
        motion = route_field(motion_slots)[slots]
        wall = WALL_SPEED * jnp.tanh(WALL_GAIN * jnp.sum(surface_normals * motion, axis=1))
        new_state = fluid_state - STEP_RATIO * (horizontal + vertical_terms(fluid_state, wall))
        pressure = state_pressure(new_state[:, 0])
        traction = -LOAD_SCALE * (pressure - PRESSURE_REF)[:, None, :] * surface_normals
        owner_traction = route_field(pack(traction))
        loads = owner_loads(kernels, owner_support, blocks, owner_traction)
        response = conjugate(estimate, struct_load + loads, operate)
        residual = response - estimate
        if count > 0:
            differences = jnp.concatenate(
                [differences[1:], (residual - last_residual)[None]], axis=0
            )
            responses = jnp.concatenate([responses[1:], (response - last_response)[None]], axis=0)
        last_residual = residual
        last_response = response
        gram = jnp.einsum("hbdp,gbdp->hg", differences, differences, precision=TOP_PRECISION)
        projected = jnp.einsum("hbdp,bdp->h", differences, residual, precision=TOP_PRECISION)
        totals = global_sums(jnp.concatenate([gram, projected[:, None]], axis=1))
        estimate = newton_update(response, totals[:, :-1], totals[:, -1], responses)
    return (new_state, estimate, residual)


def solution(mesh):
    placed = (
        P(None, None, "fx", "fy"),
        P(("fx", "fy"), None, None),
        P(("fx", "fy"), None, None),
        P(("fx", "fy"), None),
        P(("fx", "fy"), None),
        P(("fx", "fy"), None, None),
        P(("fx", "fy"), None, None, None),
        P(("fx", "fy"), None),
        P(("fx", "fy"), None),
        P(("fx", "fy"), None, None),
        P(("fx", "fy"), None, None),
        P(None, ("fx", "fy"), None, None),
        P(None, ("fx", "fy"), None, None),
    )
    return jax.shard_map(
        on_device,
        mesh=mesh,
        in_specs=placed,
        out_specs=(
            P(None, None, "fx", "fy"),
            P(("fx", "fy"), None, None),
            P(("fx", "fy"), None, None),
        ),
        check_vma=False,
    )
```

profile of v0, /device:TPU:1, one launch (start us, length us, event | category | flops | bytes accessed | tf_op | source)
XLA Modules:
  0.0 1005.2 jit_solution(8151141601063758827)
XLA Ops:
  6.5 11.5 %all-to-all-start = ((s32[128,2,2]{1,2,0:T(2,128)}), s32[128,2,2]{1,2,0:T(2,128)S(1)}, u32[]{:S(2)}, u32[]{:S(2)}) async-start(s32[128,2,2]{1,2,0:T(2,128)} %copy.261), calls=%async_computation | async-start | bytes 262144 | tf_op jit(solution)/shard_map/all_to_all | solution.py:134
  19.6 5.4 collective-permute-start.1
  32.7 12.5 %scatter_fusion = f32[256,3,128]{2,1,0:T(4,128)} fusion(f32[256,3,128]{2,1,0:T(4,128)} %broadcast.438.clone, s32[128]{0:T(128)S(1)} %fusion.166, f32[128,3,128]{2,1,0:T(4,128)S(1)} %copy.265), kind=kCustom, calls=%fused_computation.12 | custom fusion | bytes 590336 | tf_op jit(solution)/shard_map/scatter | solution.py:214
  45.2 15.0 %all-to-all-start.1 = ((f32[256,3,128]{2,1,0:T(4,128)}), f32[256,3,128]{2,1,0:T(4,128)}, u32[]{:S(2)}, u32[]{:S(2)}) async-start(f32[256,3,128]{2,1,0:T(4,128)} %scatter_fusion), calls=%async_computation.1 | async-start | bytes 1048576 | tf_op jit(solution)/shard_map/all_to_all | solution.py:133
  65.0 3.3 fusion.182
  70.4 3.3 copy.253
  75.3 3.9 copy.254
  87.1 3.2 copy.255
  90.4 3.2 copy.256
  93.6 5.9 pad_maximum_fusion
  100.7 3.1 slice_multiply_fusion
  103.8 3.0 fusion.26
  112.6 69.3 %while.20 = (s32[]{:T(128)}, f32[16,16,2,128,128]{4,3,2,1,0:T(8,128)}, f32[16,16,3,128]{3,1,2,0:T(8,128)}, s32[16,16,2]{1,0,2:T(8,128)S(1)}, f32[8,3,128]{2,1,0:T(4,128)S(1)}, /*index=5*/s32[]{:T(128)}) while((s32[]{:T(128)}, f32[16,16,2,128,128]{4,3,2,1,0:T(8,128)}, f32[16,16,3,128]{3,1,2,0:T(8,128)}, s32[16,16,2]{1,0,2:T(8,128)S(1)}, ...), condition=%wide.region_5.6_spmd, body=%wide.region_4.5_spmd.sunk | while | flops 8389730 | bytes 2471257 | solution.py:113
  114.2 2.8 fusion.215
  118.6 2.7 fusion.215
  122.9 2.7 fusion.215
  127.3 2.7 fusion.215
  135.9 2.7 fusion.215
  140.3 2.7 fusion.215
  144.6 2.7 fusion.215
  148.9 2.8 fusion.215
  153.3 2.7 fusion.215
  157.6 2.7 fusion.215
  161.9 2.7 fusion.215
  170.6 2.7 fusion.215
  179.2 2.7 fusion.215
  182.0 32.0 %convolution_bitcast_fusion.3 = f32[256,3,128]{2,1,0:T(4,128)} fusion(f32[256,2,128,128]{3,2,1,0:T(8,128)} %bitcast.465, f32[256,2,3,128]{3,1,0,2:T(2,128)S(1)} %bitcast.471), kind=kOutput, calls=%fused_computation.76 | convolution fusion | flops 301989888 | bytes 34734080 | tf_op jit(solution)/shard_map/gkij,gkcj->gci/dot_general | solution.py:120
  213.9 10.2 %all-to-all-start.2 = ((f32[256,3,128]{2,1,0:T(4,128)}), f32[256,3,128]{2,1,0:T(4,128)}, u32[]{:S(2)}, u32[]{:S(2)}) async-start(f32[256,3,128]{2,1,0:T(4,128)} %convolution_bitcast_fusion.3), calls=%async_computation.2 | async-start | bytes 1048576 | tf_op jit(solution)/shard_map/all_to_all | solution.py:140
  224.2 11.7 %fusion.4 = f32[5,8,128,129]{3,2,1,0:T(8,128)} fusion(f32[5,8,130,1]{3,2,1,0:T(8,128)} %copy.255, f32[5,8,1,128]{3,2,1,0:T(1,128)S(1)} %bitcast.482, f32[5,8,128,128]{3,2,1,0:T(8,128)} %param.40, f32[5,8,1,128]{3,2,1,0:T(1,128)S(1)} %bitcast.487, f32[5,8,130,1]{3,2,1,0:T(8,128)} %copy.256, f32[5,8,128,130]{3,2,1,0:T(8,128)} %fusion.25, f32[8,128,129]{2,1,0:T(8,128)} %fusion.24), kind=kLoop, calls=%fused_computation.29 | loop fusion | flops 7265280 | bytes 11158144 | tf_op jit(solution)/shard_map/sub | solution.py:53
  252.1 12.4 %scatter_fusion.1 = f32[256,3,128]{2,1,0:T(4,128)} fusion(f32[256,3,128]{2,1,0:T(4,128)} %broadcast.438.clone.1, s32[128]{0:T(128)S(1)} %fusion.166, f32[128,3,128]{2,1,0:T(4,128)S(1)} %copy.273), kind=kCustom, calls=%fused_computation.13 | custom fusion | bytes 590336 | tf_op jit(solution)/shard_map/scatter | solution.py:214
  264.5 9.2 all-to-all-start.3
  276.7 10.5 %all-to-all-done.3 = f32[256,3,128]{2,1,0:T(4,128)S(1)} async-done(((f32[256,3,128]{2,1,0:T(4,128)}), f32[256,3,128]{2,1,0:T(4,128)S(1)}, u32[]{:S(2)}, u32[]{:S(2)}) %all-to-all-start.3) | async-done | bytes 393248 | tf_op jit(solution)/shard_map/all_to_all | solution.py:140
  287.2 19.6 %convolution_bitcast_fusion.1 = f32[256,2,3,128]{3,2,1,0:T(4,128)S(1)} fusion(f32[256,2,128,128]{3,2,1,0:T(8,128)} %bitcast.466, f32[256,3,128]{2,1,0:T(4,128)S(1)} %all-to-all-done.3), kind=kOutput, calls=%fused_computation.74 | convolution fusion | flops 301989888 | bytes 34734080 | tf_op jit(solution)/shard_map/gkij,gci->gkcj/dot_general | solution.py:124
  314.2 71.7 %all-reduce.1 = (f32[1]{0:T(128)}, f32[1]{0:T(128)}) all-reduce(f32[1]{0:T(128)} %bitcast.55, f32[1]{0:T(128)} %bitcast.63), channel_id=1, replica_groups=mesh['fx'=16,'fy'=8] {'fx','fy'}, use_global_device_ids=true, to_apply=%region_9.10 | all-reduce | flops 2 | bytes 16 | tf_op jit(solution)/shard_map/psum | solution.py:144
  388.0 62.7 %psum.72 = f32[1]{0:T(128)} all-reduce(f32[1]{0:T(128)} %bitcast.65), channel_id=1, replica_groups=mesh['fx'=16,'fy'=8] {'fx','fy'}, use_global_device_ids=true, to_apply=%region_13.14 | all-reduce | flops 1 | bytes 8 | tf_op jit(solution)/shard_map/psum | solution.py:144
  459.2 70.4 %psum.73 = f32[1]{0:T(128)} all-reduce(f32[1]{0:T(128)} %bitcast.74), channel_id=1, replica_groups=mesh['fx'=16,'fy'=8] {'fx','fy'}, use_global_device_ids=true, to_apply=%region_15.16 | all-reduce | flops 1 | bytes 8 | tf_op jit(solution)/shard_map/psum | solution.py:144
  531.3 62.6 %psum.74 = f32[8,9]{0,1:T(8,128)S(1)} all-reduce(f32[8,9]{0,1:T(8,128)S(1)} %pad_maximum_fusion.17), channel_id=1, replica_groups=mesh['fx'=16,'fy'=8] {'fx','fy'}, use_global_device_ids=true, to_apply=%region_16.17 | all-reduce | flops 72 | bytes 576 | tf_op jit(solution)/shard_map/psum | solution.py:144
  599.2 31.6 %convolution_bitcast_fusion.2 = f32[256,3,128]{2,1,0:T(4,128)} fusion(f32[256,2,3,128]{3,2,1,0:T(4,128)S(1)} %bitcast.472, f32[256,2,128,128]{3,2,1,0:T(8,128)} %bitcast.467), kind=kOutput, calls=%fused_computation.75 | convolution fusion | flops 301989888 | bytes 34734080 | tf_op jit(solution)/shard_map/gkij,gkcj->gci/dot_general | solution.py:120
  630.9 5.4 all-to-all-start.4
  639.1 10.9 %all-to-all-done.4 = f32[256,3,128]{2,1,0:T(4,128)S(1)} async-done(((f32[256,3,128]{2,1,0:T(4,128)}), f32[256,3,128]{2,1,0:T(4,128)S(1)}, u32[]{:S(2)}, u32[]{:S(2)}) %all-to-all-start.4) | async-done | bytes 393248 | tf_op jit(solution)/shard_map/all_to_all | solution.py:140
  664.4 12.4 %scatter_fusion.2 = f32[256,3,128]{2,1,0:T(4,128)} fusion(f32[256,3,128]{2,1,0:T(4,128)} %broadcast.438, s32[128]{0:T(128)S(1)} %copy-done.27, f32[128,3,128]{2,1,0:T(4,128)S(1)} %copy.296), kind=kCustom, calls=%fused_computation.14 | custom fusion | bytes 590336 | tf_op jit(solution)/shard_map/scatter | solution.py:214
  676.8 4.6 all-to-all-start.5
  686.7 8.3 all-to-all-done.5
  695.0 19.6 %convolution_bitcast_fusion = f32[256,2,3,128]{3,2,1,0:T(4,128)S(1)} fusion(f32[256,2,128,128]{3,2,1,0:T(8,128)} %bitcast.468, f32[256,3,128]{2,1,0:T(4,128)S(1)} %all-to-all-done.5), kind=kOutput, calls=%fused_computation.73 | convolution fusion | flops 301989888 | bytes 34734080 | tf_op jit(solution)/shard_map/gkij,gci->gkcj/dot_general | solution.py:124
  721.3 71.7 %all-reduce = (f32[1]{0:T(128)}, f32[1]{0:T(128)}) all-reduce(f32[1]{0:T(128)} %bitcast.119, f32[1]{0:T(128)} %bitcast.127), channel_id=1, replica_groups=mesh['fx'=16,'fy'=8] {'fx','fy'}, use_global_device_ids=true, to_apply=%region_22.26 | all-reduce | flops 2 | bytes 16 | tf_op jit(solution)/shard_map/psum | solution.py:144
  795.0 62.5 %psum.77 = f32[1]{0:T(128)} all-reduce(f32[1]{0:T(128)} %bitcast.129), channel_id=1, replica_groups=mesh['fx'=16,'fy'=8] {'fx','fy'}, use_global_device_ids=true, to_apply=%region_26.30 | all-reduce | flops 1 | bytes 8 | tf_op jit(solution)/shard_map/psum | solution.py:144
  866.1 70.4 %psum.78 = f32[1]{0:T(128)} all-reduce(f32[1]{0:T(128)} %bitcast.138), channel_id=1, replica_groups=mesh['fx'=16,'fy'=8] {'fx','fy'}, use_global_device_ids=true, to_apply=%region_28.32 | all-reduce | flops 1 | bytes 8 | tf_op jit(solution)/shard_map/psum | solution.py:144
  938.5 62.6 %psum.79 = f32[8,9]{0,1:T(8,128)S(1)} all-reduce(f32[8,9]{0,1:T(8,128)S(1)} %pad_maximum_fusion.18), channel_id=1, replica_groups=mesh['fx'=16,'fy'=8] {'fx','fy'}, use_global_device_ids=true, to_apply=%region_29.33 | all-reduce | flops 72 | bytes 576 | tf_op jit(solution)/shard_map/psum | solution.py:144
  (398 shorter events, 153.0 us)
Async XLA Ops:
  0.6 24.4 %copy-start = (f32[8,4,128,128]{3,2,1,0:T(8,128)S(1)}, f32[8,4,128,128]{3,2,1,0:T(8,128)}, u32[]{:S(2)}) copy-start(f32[8,4,128,128]{3,2,1,0:T(8,128)} %param.46) | copy-start | bytes 6291460
  0.6 27.7 %copy-start.1 = (f32[8,3,128]{2,0,1:T(8,128)S(1)}, f32[8,3,128]{2,0,1:T(8,128)}, u32[]{:S(2)}) copy-start(f32[8,3,128]{2,0,1:T(8,128)} %param.50) | copy-start | bytes 36868
  0.7 26.2 %copy-start.20 = (s32[8,4]{0,1:T(4,128)S(1)}, s32[8,4]{0,1:T(4,128)}, u32[]{:S(2)}) copy-start(s32[8,4]{0,1:T(4,128)} %param.47) | copy-start | bytes 388
  0.7 30.9 %copy-start.18 = (f32[128,3,128]{2,0,1:T(8,128)S(1)}, f32[128,3,128]{2,0,1:T(8,128)}, u32[]{:S(2)}) copy-start(f32[128,3,128]{2,0,1:T(8,128)} %param.41) | copy-start | bytes 589828
  1.7 29.9 %copy-start.25 = (f32[8,3,128]{2,0,1:T(8,128)S(1)}, f32[8,3,128]{2,0,1:T(8,128)}, u32[]{:S(2)}) copy-start(f32[8,3,128]{2,0,1:T(8,128)} %param.45) | copy-start | bytes 36868
  3.3 248.8 %copy-start.26 = (s32[128]{0:T(128)}, s32[128]{0:T(128)S(1)}, u32[]{:S(2)}) copy-start(s32[128]{0:T(128)S(1)} %fusion.166) | copy-start | bytes 1540
  6.5 38.7 %all-to-all-start = ((s32[128,2,2]{1,2,0:T(2,128)}), s32[128,2,2]{1,2,0:T(2,128)S(1)}, u32[]{:S(2)}, u32[]{:S(2)}) async-start(s32[128,2,2]{1,2,0:T(2,128)} %copy.261), calls=%async_computation | async-start | bytes 262144 | tf_op jit(solution)/shard_map/all_to_all | solution.py:134
  19.6 43.4 %collective-permute-start.1 = (f32[5,8,1,128]{3,1,2,0:T(8,128)}, f32[5,8,1,128]{3,1,2,0:T(8,128)S(1)}, u32[]{:S(2)}, u32[]{:S(2)}) collective-permute-start(f32[5,8,1,128]{3,1,2,0:T(8,128)} %bitcast.176), channel_id=1, source_target_pairs={{8,0},{16,8},{24,16},{32,24},{40,32},{48,40},{56,48},{64,56},{72,6... | collective-permute-start | bytes 61448 | tf_op jit(solution)/shard_map/ppermute | solution.py:27
  25.0 38.0 %collective-permute-start = (f32[5,8,1,128]{3,1,2,0:T(8,128)}, f32[5,8,1,128]{3,1,2,0:T(8,128)S(1)}, u32[]{:S(2)}, u32[]{:S(2)}) collective-permute-start(f32[5,8,1,128]{3,1,2,0:T(8,128)} %bitcast.175), channel_id=1, source_target_pairs={{0,8},{8,16},{16,24},{24,32},{32,40},{40,48},{48,56},{56,64},{64,7... | collective-permute-start | bytes 61448 | tf_op jit(solution)/shard_map/ppermute | solution.py:25
  27.7 279.1 %collective-permute-start.5 = (f32[8,3,128]{2,0,1:T(8,128)}, f32[8,3,128]{2,0,1:T(8,128)}, u32[]{:S(2)}, u32[]{:S(2)}) collective-permute-start(f32[8,3,128]{2,0,1:T(8,128)} %convolution_bitcast_fusion.22), channel_id=1, source_target_pairs={{1,0},{2,1},{3,2},{4,3},{5,4},{6,5},{7,6},{8,7},{9,8},{10,9},{11,1... | collective-permute-start | bytes 36872 | tf_op jit(solution)/shard_map/ppermute | solution.py:27
  28.3 245.9 %collective-permute-start.4 = (f32[8,3,128]{2,1,0:T(4,128)S(1)}, f32[8,3,128]{2,1,0:T(4,128)S(1)}, u32[]{:S(2)}, u32[]{:S(2)}) collective-permute-start(f32[8,3,128]{2,1,0:T(4,128)S(1)} %copy.275), channel_id=1, source_target_pairs={{0,1},{1,2},{2,3},{3,4},{4,5},{5,6},{6,7},{7,8},{8,9},{9,10},{10,1... | collective-permute-start | bytes 36872 | tf_op jit(solution)/shard_map/ppermute | solution.py:25
  30.7 30.1 %copy-start.9 = (f32[5,1,128,128]{3,2,1,0:T(8,128)}, f32[5,1,128,128]{3,2,1,0:T(8,128)S(1)}, u32[]{:S(2)}) copy-start(f32[5,1,128,128]{3,2,1,0:T(8,128)S(1)} %get-tuple-element.226) | copy-start | bytes 983044
  30.7 206.5 %copy-start.28 = (s32[1024]{0:T(1024)}, s32[1024]{0:T(1024)S(1)}, u32[]{:S(2)}) copy-start(s32[1024]{0:T(1024)S(1)} %pad_clamp_fusion.2) | copy-start | bytes 12292
  45.2 65.6 %all-to-all-start.1 = ((f32[256,3,128]{2,1,0:T(4,128)}), f32[256,3,128]{2,1,0:T(4,128)}, u32[]{:S(2)}, u32[]{:S(2)}) async-start(f32[256,3,128]{2,1,0:T(4,128)} %scatter_fusion), calls=%async_computation.1 | async-start | bytes 1048576 | tf_op jit(solution)/shard_map/all_to_all | solution.py:133
  65.0 4.2 copy-start.5
  73.7 13.5 %collective-permute-start.2 = (f32[5,8,130,1]{2,1,3,0:T(8,128)S(1)}, f32[5,8,130,1]{2,1,3,0:T(8,128)}, u32[]{:S(2)}, u32[]{:S(2)}) collective-permute-start(f32[5,8,130,1]{2,1,3,0:T(8,128)S(1)} %copy.253), channel_id=1, source_target_pairs={{0,1},{1,2},{2,3},{3,4},{4,5},{5,6},{6,7},{7,0},{8,9},{9,10},{10,1... | collective-permute-start | bytes 62408 | tf_op jit(solution)/shard_map/ppermute | solution.py:25
  79.2 2.7 copy-start.6
  79.2 11.2 %collective-permute-start.3 = (f32[5,8,130,1]{2,1,3,0:T(8,128)}, f32[5,8,130,1]{2,1,3,0:T(8,128)}, u32[]{:S(2)}, u32[]{:S(2)}) collective-permute-start(f32[5,8,130,1]{2,1,3,0:T(8,128)} %copy.254), channel_id=1, source_target_pairs={{1,0},{2,1},{3,2},{4,3},{5,4},{6,5},{7,6},{0,7},{9,8},{10,9},{11,1... | collective-permute-start | bytes 62408 | tf_op jit(solution)/shard_map/ppermute | solution.py:27
  213.9 23.2 %all-to-all-start.2 = ((f32[256,3,128]{2,1,0:T(4,128)}), f32[256,3,128]{2,1,0:T(4,128)}, u32[]{:S(2)}, u32[]{:S(2)}) async-start(f32[256,3,128]{2,1,0:T(4,128)} %convolution_bitcast_fusion.3), calls=%async_computation.2 | async-start | bytes 1048576 | tf_op jit(solution)/shard_map/all_to_all | solution.py:140
  224.2 14.8 %copy-start.14 = (f32[128,3,128]{2,0,1:T(8,128)S(1)}, f32[128,3,128]{2,0,1:T(8,128)}, u32[]{:S(2)}) copy-start(f32[128,3,128]{2,0,1:T(8,128)} %param.42) | copy-start | bytes 589828
  224.2 15.1 %copy-start.10 = (f32[5,1,128,128]{3,2,1,0:T(8,128)S(1)}, f32[5,1,128,128]{3,2,1,0:T(8,128)}, u32[]{:S(2)}) copy-start(f32[5,1,128,128]{3,2,1,0:T(8,128)} %copy-done.9) | copy-start | bytes 983044
  245.1 2.2 slice-start
  245.5 2.7 copy-start.7
  245.5 3.0 slice-start.1
  251.0 22.8 %copy-start.16 = (f32[8,8,3,128]{3,1,2,0:T(8,128)S(1)}, f32[8,8,3,128]{3,1,2,0:T(8,128)}, u32[]{:S(2)}) copy-start(f32[8,8,3,128]{3,1,2,0:T(8,128)} %param.51) | copy-start | bytes 294916
  264.5 22.7 %all-to-all-start.3 = ((f32[256,3,128]{2,1,0:T(4,128)}), f32[256,3,128]{2,1,0:T(4,128)S(1)}, u32[]{:S(2)}, u32[]{:S(2)}) async-start(f32[256,3,128]{2,1,0:T(4,128)} %scatter_fusion.1), calls=%async_computation.3 | async-start | bytes 1048576 | tf_op jit(solution)/shard_map/all_to_all | solution.py:140
  274.3 32.6 %copy-start.23 = (s32[256,2]{0,1:T(2,128)}, s32[256,2]{0,1:T(2,128)S(1)}, u32[]{:S(2)}) copy-start(s32[256,2]{0,1:T(2,128)S(1)} %eq.26) | copy-start | bytes 6148
  276.7 30.1 %copy-start.19 = (f32[8,128]{1,0:T(8,128)S(1)}, f32[8,128]{1,0:T(8,128)}, u32[]{:S(2)}) copy-start(f32[8,128]{1,0:T(8,128)} %param.48) | copy-start | bytes 12292
  276.7 30.1 %copy-start.22 = (f32[8,3,128]{2,0,1:T(8,128)S(1)}, f32[8,3,128]{2,0,1:T(8,128)}, u32[]{:S(2)}) copy-start(f32[8,3,128]{2,0,1:T(8,128)} %param.49) | copy-start | bytes 36868
  308.0 2.5 collective-permute-start.6
  310.5 3.1 collective-permute-start.7
  312.9 283.9 %copy-start.17 = (f32[8,8,3,128]{3,1,2,0:T(8,128)S(1)}, f32[8,8,3,128]{3,1,2,0:T(8,128)}, u32[]{:S(2)}) copy-start(f32[8,8,3,128]{3,1,2,0:T(8,128)} %param.52) | copy-start | bytes 294916
  452.1 3.0 collective-permute-start.8
  455.1 3.4 collective-permute-start.9
  630.9 19.1 %all-to-all-start.4 = ((f32[256,3,128]{2,1,0:T(4,128)}), f32[256,3,128]{2,1,0:T(4,128)S(1)}, u32[]{:S(2)}, u32[]{:S(2)}) async-start(f32[256,3,128]{2,1,0:T(4,128)} %convolution_bitcast_fusion.2), calls=%async_computation.4 | async-start | bytes 1048576 | tf_op jit(solution)/shard_map/all_to_all | solution.py:140
  637.1 47.1 %collective-permute-start.10 = (f32[8,3,128]{2,0,1:T(8,128)S(1)}, f32[8,3,128]{2,0,1:T(8,128)S(1)}, u32[]{:S(2)}, u32[]{:S(2)}) collective-permute-start(f32[8,3,128]{2,0,1:T(8,128)S(1)} %bitcast_subtract_fusion.1), channel_id=1, source_target_pairs={{0,1},{1,2},{2,3},{3,4},{4,5},{5,6},{6,7},{7,8},{8,9},{9,10},{10,1... | collective-permute-start | bytes 36872 | tf_op jit(solution)/shard_map/ppermute | solution.py:25
  655.7 1.8 copy-start.11
  660.7 2.6 copy-start.15
  660.7 3.7 copy-start.27
  676.8 18.1 %all-to-all-start.5 = ((f32[256,3,128]{2,1,0:T(4,128)}), f32[256,3,128]{2,1,0:T(4,128)S(1)}, u32[]{:S(2)}, u32[]{:S(2)}) async-start(f32[256,3,128]{2,1,0:T(4,128)} %scatter_fusion.2), calls=%async_computation.5 | async-start | bytes 1048576 | tf_op jit(solution)/shard_map/all_to_all | solution.py:140
  682.8 31.9 %collective-permute-start.11 = (f32[8,3,128]{2,0,1:T(8,128)S(1)}, f32[8,3,128]{2,0,1:T(8,128)S(1)}, u32[]{:S(2)}, u32[]{:S(2)}) collective-permute-start(f32[8,3,128]{2,0,1:T(8,128)S(1)} %convolution_bitcast_fusion.18), channel_id=1, source_target_pairs={{1,0},{2,1},{3,2},{4,3},{5,4},{6,5},{7,6},{8,7},{9,8},{10,9},{11,1... | collective-permute-start | bytes 36872 | tf_op jit(solution)/shard_map/ppermute | solution.py:27
  686.7 28.0 %copy-start.24 = (s32[256,2]{0,1:T(2,128)S(1)}, s32[256,2]{0,1:T(2,128)}, u32[]{:S(2)}) copy-start(s32[256,2]{0,1:T(2,128)} %copy-done.23) | copy-start | bytes 6148
  715.1 2.5 collective-permute-start.12
  717.5 3.1 collective-permute-start.13
  720.0 284.1 %slice-start.2 = ((f32[8,8,3,128]{3,1,2,0:T(8,128)}), f32[7,8,3,128]{3,1,2,0:T(8,128)S(1)}, s32[]{:S(2)}) async-start(f32[8,8,3,128]{3,1,2,0:T(8,128)} %param.52), calls=%async_computation.8 | async-start | bytes 172032 | tf_op jit(solution)/shard_map/slice | solution.py:249
  858.9 3.2 collective-permute-start.14
  862.0 3.4 collective-permute-start.15
  937.8 67.2 %copy-start.21 = (f32[8,3,128]{2,0,1:T(8,128)}, f32[8,3,128]{2,0,1:T(8,128)S(1)}, u32[]{:S(2)}) copy-start(f32[8,3,128]{2,0,1:T(8,128)S(1)} %get-tuple-element.201) | copy-start | bytes 36868
  (6 other events, 9.5 us)
where the time goes:
time: 1010 us
  blocking collectives  535 us (53%)
  matrix products  127 us (13%)
  local copies, waits for them, and re-layouts  113 us (11%)
  other arithmetic  113 us (11%)
  starting transfers between devices  74.2 us (7%)
  waiting for transfers between devices  34.2 us (3%)
    psum x8, blocking collectives, global_sums(): return lax.psum(values, ('fx', 'fy'))  535 us
    dot_general x2, matrix products, owner_motion(): jnp.einsum('gkij,gkcj->gci', kernels, field_values[support], precision=TO...  63.6 us
    dynamic_update_slice x16, other arithmetic, owner_kernels(): lax.map(one_group, (places.reshape(-1, group, 3, points), support.reshape...  43.5 us
    dot_general x2, matrix products, owner_loads(): jnp.einsum('gkij,gci->gkcj', kernels, traction, precision=TOP_PRECISION)  39.3 us
    scatter x4, local copies, waits for them, and re-layouts, pack(): jnp.zeros((width,) + values.shape[1:], values.dtype).at[slots].set(values)  38.3 us
    all_to_all x4, waiting for transfers between devices, route_field(): lax.all_to_all(values, ('fx', 'fy'), split_axis=0, concat_axis=0, tiled=T...  30.9 us
    all_to_all x4, starting transfers between devices, route_field(): lax.all_to_all(values, ('fx', 'fy'), split_axis=0, concat_axis=0, tiled=T...  29.5 us
  transfers between devices with their start and end apart: 22, of which 8 were waited for; matrix products, arithmetic and copies ran while one was open for 29% of the time, Pallas kernels for 0%

commit v1 on v0

--- a/solution.py
+++ b/solution.py
@@ -141,7 +141,7 @@
 
 
 def global_sums(values):
-    return lax.psum(values, ("fx", "fy"))
+    return lax.psum(lax.psum(values, "fx"), "fy")
 
 
 def stiffness(field_values, couplings, sparsity_layout, selector, diagonal):

time: 1010 us -> 899 us (0.89)
  blocking collectives: 535 us -> 425 us
    psum x8 -> x16, blocking collectives: 535 us -> 425 us  [global_sums(): return lax.psum(lax.psum(values, 'fx'), 'fy')]
  transfers between devices with their start and end apart: 22 -> 22, of which waited for: 8 -> 6; matrix products, arithmetic and copies ran while one was open for 29% -> 32% of each run, Pallas kernels for 0% -> 0%
where the time goes in v1:
time: 899 us; the launch traced here: 891 us
  blocking collectives  425 us (47%)
  matrix products  127 us (14%)
  other arithmetic  113 us (13%)
  local copies, waits for them, and re-layouts  112 us (12%)
  starting transfers between devices  70.8 us (8%)
  waiting for transfers between devices  33.6 us (4%)
  between operations  9.95 us (1%)
    psum x16, blocking collectives, global_sums(): return lax.psum(lax.psum(values, 'fx'), 'fy')  425 us
    dot_general x2, matrix products, owner_motion(): jnp.einsum('gkij,gkcj->gci', kernels, field_values[support], precision=TO...  63.6 us
    dynamic_update_slice x16, other arithmetic, owner_kernels(): lax.map(one_group, (places.reshape(-1, group, 3, points), support.reshape...  43.5 us
    dot_general x2, matrix products, owner_loads(): jnp.einsum('gkij,gci->gkcj', kernels, traction, precision=TOP_PRECISION)  39.3 us
    scatter x4, local copies, waits for them, and re-layouts, pack(): jnp.zeros((width,) + values.shape[1:], values.dtype).at[slots].set(values)  38.3 us
    all_to_all x4, waiting for transfers between devices, route_field(): lax.all_to_all(values, ('fx', 'fy'), split_axis=0, concat_axis=0, tiled=T...  32.2 us
    all_to_all x4, starting transfers between devices, route_field(): lax.all_to_all(values, ('fx', 'fy'), split_axis=0, concat_axis=0, tiled=T...  28 us
  transfers between devices with their start and end apart: 22, of which 6 were waited for; matrix products, arithmetic and copies ran while one was open for 32% of the time, Pallas kernels for 0%

profile of v1, /device:TPU:1, one launch (start us, length us, event | category | flops | bytes accessed | tf_op | source)
XLA Modules:
  0.0 890.9 jit_solution(4745343657798626561)
XLA Ops:
  6.5 11.5 %all-to-all-start = ((s32[128,2,2]{1,2,0:T(2,128)}), s32[128,2,2]{1,2,0:T(2,128)S(1)}, u32[]{:S(2)}, u32[]{:S(2)}) async-start(s32[128,2,2]{1,2,0:T(2,128)} %copy.261), calls=%async_computation | async-start | bytes 262144 | tf_op jit(solution)/shard_map/all_to_all | solution.py:134
  19.6 5.4 collective-permute-start.1
  32.5 12.5 %scatter_fusion = f32[256,3,128]{2,1,0:T(4,128)} fusion(f32[256,3,128]{2,1,0:T(4,128)} %broadcast.438.clone, s32[128]{0:T(128)S(1)} %fusion.166, f32[128,3,128]{2,1,0:T(4,128)S(1)} %copy.265), kind=kCustom, calls=%fused_computation.12 | custom fusion | bytes 590336 | tf_op jit(solution)/shard_map/scatter | solution.py:214
  45.0 14.9 %all-to-all-start.1 = ((f32[256,3,128]{2,1,0:T(4,128)}), f32[256,3,128]{2,1,0:T(4,128)}, u32[]{:S(2)}, u32[]{:S(2)}) async-start(f32[256,3,128]{2,1,0:T(4,128)} %scatter_fusion), calls=%async_computation.1 | async-start | bytes 1048576 | tf_op jit(solution)/shard_map/all_to_all | solution.py:133
  64.7 3.3 fusion.182
  70.1 3.3 copy.253
  75.0 3.9 copy.254
  86.9 3.2 copy.255
  90.1 3.2 copy.256
  93.3 5.9 pad_maximum_fusion
  100.4 3.1 slice_multiply_fusion
  103.5 3.0 fusion.26
  112.3 69.4 %while.20 = (s32[]{:T(128)}, f32[16,16,2,128,128]{4,3,2,1,0:T(8,128)}, f32[16,16,3,128]{3,1,2,0:T(8,128)}, s32[16,16,2]{1,0,2:T(8,128)S(1)}, f32[8,3,128]{2,1,0:T(4,128)S(1)}, /*index=5*/s32[]{:T(128)}) while((s32[]{:T(128)}, f32[16,16,2,128,128]{4,3,2,1,0:T(8,128)}, f32[16,16,3,128]{3,1,2,0:T(8,128)}, s32[16,16,2]{1,0,2:T(8,128)S(1)}, ...), condition=%wide.region_5.6_spmd, body=%wide.region_4.5_spmd.sunk | while | flops 8389730 | bytes 2471257 | solution.py:113
  114.0 2.8 fusion.215
  122.7 2.7 fusion.215
  148.6 2.8 fusion.215
  157.4 2.7 fusion.215
  179.0 2.7 fusion.215
  181.7 32.0 %convolution_bitcast_fusion.3 = f32[256,3,128]{2,1,0:T(4,128)} fusion(f32[256,2,128,128]{3,2,1,0:T(8,128)} %bitcast.465, f32[256,2,3,128]{3,1,0,2:T(2,128)S(1)} %bitcast.471), kind=kOutput, calls=%fused_computation.76 | convolution fusion | flops 301989888 | bytes 34734080 | tf_op jit(solution)/shard_map/gkij,gkcj->gci/dot_general | solution.py:120
  213.7 10.2 %all-to-all-start.2 = ((f32[256,3,128]{2,1,0:T(4,128)}), f32[256,3,128]{2,1,0:T(4,128)}, u32[]{:S(2)}, u32[]{:S(2)}) async-start(f32[256,3,128]{2,1,0:T(4,128)} %convolution_bitcast_fusion.3), calls=%async_computation.2 | async-start | bytes 1048576 | tf_op jit(solution)/shard_map/all_to_all | solution.py:140
  224.0 11.7 %fusion.4 = f32[5,8,128,129]{3,2,1,0:T(8,128)} fusion(f32[5,8,130,1]{3,2,1,0:T(8,128)} %copy.255, f32[5,8,1,128]{3,2,1,0:T(1,128)S(1)} %bitcast.482, f32[5,8,128,128]{3,2,1,0:T(8,128)} %param.40, f32[5,8,1,128]{3,2,1,0:T(1,128)S(1)} %bitcast.487, f32[5,8,130,1]{3,2,1,0:T(8,128)} %copy.256, f32[5,8,128,130]{3,2,1,0:T(8,128)} %fusion.25, f32[8,128,129]{2,1,0:T(8,128)} %fusion.24), kind=kLoop, calls=%fused_computation.29 | loop fusion | flops 7265280 | bytes 11158144 | tf_op jit(solution)/shard_map/sub | solution.py:53
  251.8 12.5 %scatter_fusion.1 = f32[256,3,128]{2,1,0:T(4,128)} fusion(f32[256,3,128]{2,1,0:T(4,128)} %broadcast.438.clone.1, s32[128]{0:T(128)S(1)} %fusion.166, f32[128,3,128]{2,1,0:T(4,128)S(1)} %copy.273), kind=kCustom, calls=%fused_computation.13 | custom fusion | bytes 590336 | tf_op jit(solution)/shard_map/scatter | solution.py:214
  264.3 9.2 %all-to-all-start.3 = ((f32[256,3,128]{2,1,0:T(4,128)}), f32[256,3,128]{2,1,0:T(4,128)S(1)}, u32[]{:S(2)}, u32[]{:S(2)}) async-start(f32[256,3,128]{2,1,0:T(4,128)} %scatter_fusion.1), calls=%async_computation.3 | async-start | bytes 1048576 | tf_op jit(solution)/shard_map/all_to_all | solution.py:140
  276.2 10.6 %all-to-all-done.3 = f32[256,3,128]{2,1,0:T(4,128)S(1)} async-done(((f32[256,3,128]{2,1,0:T(4,128)}), f32[256,3,128]{2,1,0:T(4,128)S(1)}, u32[]{:S(2)}, u32[]{:S(2)}) %all-to-all-start.3) | async-done | bytes 393248 | tf_op jit(solution)/shard_map/all_to_all | solution.py:140
  286.9 19.6 %convolution_bitcast_fusion.1 = f32[256,2,3,128]{3,2,1,0:T(4,128)S(1)} fusion(f32[256,2,128,128]{3,2,1,0:T(8,128)} %bitcast.466, f32[256,3,128]{2,1,0:T(4,128)S(1)} %all-to-all-done.3), kind=kOutput, calls=%fused_computation.74 | convolution fusion | flops 301989888 | bytes 34734080 | tf_op jit(solution)/shard_map/gkij,gci->gkcj/dot_general | solution.py:124
  313.9 30.5 %all-reduce.1 = (f32[1]{0:T(128)}, f32[1]{0:T(128)}) all-reduce(f32[1]{0:T(128)} %bitcast.55, f32[1]{0:T(128)} %bitcast.63), channel_id=1, replica_groups=mesh['fx'=16,'fy'=8] {'fx'}, use_global_device_ids=true, to_apply=%region_9.10 | all-reduce | flops 2 | bytes 16 | tf_op jit(solution)/shard_map/psum | solution.py:144
  344.4 24.7 %all-reduce.3 = (f32[1]{0:T(128)}, f32[1]{0:T(128)}) all-reduce(f32[1]{0:T(128)} %get-tuple-element.196, f32[1]{0:T(128)} %get-tuple-element.197), channel_id=1, replica_groups=mesh['fx'=16,'fy'=8] {'fy'}, use_global_device_ids=true, to_apply=%region_10.11 | all-reduce | flops 2 | bytes 16 | tf_op jit(solution)/shard_map/psum | solution.py:144
  371.0 30.9 %psum.144 = f32[1]{0:T(128)} all-reduce(f32[1]{0:T(128)} %bitcast.65), channel_id=1, replica_groups=mesh['fx'=16,'fy'=8] {'fx'}, use_global_device_ids=true, to_apply=%region_15.16 | all-reduce | flops 1 | bytes 8 | tf_op jit(solution)/shard_map/psum | solution.py:144
  401.9 20.3 %psum.145 = f32[1]{0:T(128)} all-reduce(f32[1]{0:T(128)} %psum.144), channel_id=1, replica_groups=mesh['fx'=16,'fy'=8] {'fy'}, use_global_device_ids=true, to_apply=%region_16.17 | all-reduce | flops 1 | bytes 8 | tf_op jit(solution)/shard_map/psum | solution.py:144
  428.8 29.3 %psum.146 = f32[1]{0:T(128)} all-reduce(f32[1]{0:T(128)} %bitcast.74), channel_id=1, replica_groups=mesh['fx'=16,'fy'=8] {'fx'}, use_global_device_ids=true, to_apply=%region_18.19 | all-reduce | flops 1 | bytes 8 | tf_op jit(solution)/shard_map/psum | solution.py:144
  458.4 26.5 %psum.147 = f32[1]{0:T(128)} all-reduce(f32[1]{0:T(128)} %psum.146), channel_id=1, replica_groups=mesh['fx'=16,'fy'=8] {'fy'}, use_global_device_ids=true, to_apply=%region_19.20 | all-reduce | flops 1 | bytes 8 | tf_op jit(solution)/shard_map/psum | solution.py:144
  486.6 31.0 %psum.148 = f32[8,9]{0,1:T(8,128)S(1)} all-reduce(f32[8,9]{0,1:T(8,128)S(1)} %pad_maximum_fusion.17), channel_id=1, replica_groups=mesh['fx'=16,'fy'=8] {'fx'}, use_global_device_ids=true, to_apply=%region_20.21 | all-reduce | flops 72 | bytes 576 | tf_op jit(solution)/shard_map/psum | solution.py:144
  517.7 19.6 %psum.149 = f32[8,9]{0,1:T(8,128)S(1)} all-reduce(f32[8,9]{0,1:T(8,128)S(1)} %psum.148), channel_id=1, replica_groups=mesh['fx'=16,'fy'=8] {'fy'}, use_global_device_ids=true, to_apply=%region_21.22 | all-reduce | flops 72 | bytes 576 | tf_op jit(solution)/shard_map/psum | solution.py:144
  542.6 31.6 %convolution_bitcast_fusion.2 = f32[256,3,128]{2,1,0:T(4,128)} fusion(f32[256,2,3,128]{3,2,1,0:T(4,128)S(1)} %bitcast.472, f32[256,2,128,128]{3,2,1,0:T(8,128)} %bitcast.467), kind=kOutput, calls=%fused_computation.75 | convolution fusion | flops 301989888 | bytes 34734080 | tf_op jit(solution)/shard_map/gkij,gkcj->gci/dot_general | solution.py:120
  574.3 4.1 all-to-all-start.4
  580.3 11.9 %all-to-all-done.4 = f32[256,3,128]{2,1,0:T(4,128)S(1)} async-done(((f32[256,3,128]{2,1,0:T(4,128)}), f32[256,3,128]{2,1,0:T(4,128)S(1)}, u32[]{:S(2)}, u32[]{:S(2)}) %all-to-all-start.4) | async-done | bytes 393248 | tf_op jit(solution)/shard_map/all_to_all | solution.py:140
  606.6 12.5 %scatter_fusion.2 = f32[256,3,128]{2,1,0:T(4,128)} fusion(f32[256,3,128]{2,1,0:T(4,128)} %broadcast.438, s32[128]{0:T(128)S(1)} %copy-done.27, f32[128,3,128]{2,1,0:T(4,128)S(1)} %copy.296), kind=kCustom, calls=%fused_computation.14 | custom fusion | bytes 590336 | tf_op jit(solution)/shard_map/scatter | solution.py:214
  619.1 4.5 all-to-all-start.5
  628.7 8.4 all-to-all-done.5
  637.1 19.6 %convolution_bitcast_fusion = f32[256,2,3,128]{3,2,1,0:T(4,128)S(1)} fusion(f32[256,2,128,128]{3,2,1,0:T(8,128)} %bitcast.468, f32[256,3,128]{2,1,0:T(4,128)S(1)} %all-to-all-done.5), kind=kOutput, calls=%fused_computation.73 | convolution fusion | flops 301989888 | bytes 34734080 | tf_op jit(solution)/shard_map/gkij,gci->gkcj/dot_general | solution.py:124
  663.4 30.4 %all-reduce = (f32[1]{0:T(128)}, f32[1]{0:T(128)}) all-reduce(f32[1]{0:T(128)} %bitcast.119, f32[1]{0:T(128)} %bitcast.127), channel_id=1, replica_groups=mesh['fx'=16,'fy'=8] {'fx'}, use_global_device_ids=true, to_apply=%region_27.31 | all-reduce | flops 2 | bytes 16 | tf_op jit(solution)/shard_map/psum | solution.py:144
  693.8 24.6 %all-reduce.2 = (f32[1]{0:T(128)}, f32[1]{0:T(128)}) all-reduce(f32[1]{0:T(128)} %get-tuple-element.194, f32[1]{0:T(128)} %get-tuple-element.195), channel_id=1, replica_groups=mesh['fx'=16,'fy'=8] {'fy'}, use_global_device_ids=true, to_apply=%region_28.32 | all-reduce | flops 2 | bytes 16 | tf_op jit(solution)/shard_map/psum | solution.py:144
  720.5 30.8 %psum.154 = f32[1]{0:T(128)} all-reduce(f32[1]{0:T(128)} %bitcast.129), channel_id=1, replica_groups=mesh['fx'=16,'fy'=8] {'fx'}, use_global_device_ids=true, to_apply=%region_33.37 | all-reduce | flops 1 | bytes 8 | tf_op jit(solution)/shard_map/psum | solution.py:144
  751.3 20.3 %psum.155 = f32[1]{0:T(128)} all-reduce(f32[1]{0:T(128)} %psum.154), channel_id=1, replica_groups=mesh['fx'=16,'fy'=8] {'fy'}, use_global_device_ids=true, to_apply=%region_34.38 | all-reduce | flops 1 | bytes 8 | tf_op jit(solution)/shard_map/psum | solution.py:144
  778.3 29.2 %psum.156 = f32[1]{0:T(128)} all-reduce(f32[1]{0:T(128)} %bitcast.138), channel_id=1, replica_groups=mesh['fx'=16,'fy'=8] {'fx'}, use_global_device_ids=true, to_apply=%region_36.40 | all-reduce | flops 1 | bytes 8 | tf_op jit(solution)/shard_map/psum | solution.py:144
  807.5 26.4 %psum.157 = f32[1]{0:T(128)} all-reduce(f32[1]{0:T(128)} %psum.156), channel_id=1, replica_groups=mesh['fx'=16,'fy'=8] {'fy'}, use_global_device_ids=true, to_apply=%region_37.41 | all-reduce | flops 1 | bytes 8 | tf_op jit(solution)/shard_map/psum | solution.py:144
  835.9 31.0 %psum.158 = f32[8,9]{0,1:T(8,128)S(1)} all-reduce(f32[8,9]{0,1:T(8,128)S(1)} %pad_maximum_fusion.18), channel_id=1, replica_groups=mesh['fx'=16,'fy'=8] {'fx'}, use_global_device_ids=true, to_apply=%region_38.42 | all-reduce | flops 72 | bytes 576 | tf_op jit(solution)/shard_map/psum | solution.py:144
  867.0 19.6 %psum.159 = f32[8,9]{0,1:T(8,128)S(1)} all-reduce(f32[8,9]{0,1:T(8,128)S(1)} %psum.158), channel_id=1, replica_groups=mesh['fx'=16,'fy'=8] {'fy'}, use_global_device_ids=true, to_apply=%region_39.43 | all-reduce | flops 72 | bytes 576 | tf_op jit(solution)/shard_map/psum | solution.py:144
  (407 shorter events, 170.2 us)
Async XLA Ops:
  0.6 24.4 %copy-start = (f32[8,4,128,128]{3,2,1,0:T(8,128)S(1)}, f32[8,4,128,128]{3,2,1,0:T(8,128)}, u32[]{:S(2)}) copy-start(f32[8,4,128,128]{3,2,1,0:T(8,128)} %param.46) | copy-start | bytes 6291460
  0.6 27.7 %copy-start.1 = (f32[8,3,128]{2,0,1:T(8,128)S(1)}, f32[8,3,128]{2,0,1:T(8,128)}, u32[]{:S(2)}) copy-start(f32[8,3,128]{2,0,1:T(8,128)} %param.50) | copy-start | bytes 36868
  0.7 26.2 %copy-start.20 = (s32[8,4]{0,1:T(4,128)S(1)}, s32[8,4]{0,1:T(4,128)}, u32[]{:S(2)}) copy-start(s32[8,4]{0,1:T(4,128)} %param.47) | copy-start | bytes 388
  0.7 30.8 %copy-start.18 = (f32[128,3,128]{2,0,1:T(8,128)S(1)}, f32[128,3,128]{2,0,1:T(8,128)}, u32[]{:S(2)}) copy-start(f32[128,3,128]{2,0,1:T(8,128)} %param.41) | copy-start | bytes 589828
  1.7 29.9 %copy-start.25 = (f32[8,3,128]{2,0,1:T(8,128)S(1)}, f32[8,3,128]{2,0,1:T(8,128)}, u32[]{:S(2)}) copy-start(f32[8,3,128]{2,0,1:T(8,128)} %param.45) | copy-start | bytes 36868
  3.3 248.6 %copy-start.26 = (s32[128]{0:T(128)}, s32[128]{0:T(128)S(1)}, u32[]{:S(2)}) copy-start(s32[128]{0:T(128)S(1)} %fusion.166) | copy-start | bytes 1540
  6.5 38.6 %all-to-all-start = ((s32[128,2,2]{1,2,0:T(2,128)}), s32[128,2,2]{1,2,0:T(2,128)S(1)}, u32[]{:S(2)}, u32[]{:S(2)}) async-start(s32[128,2,2]{1,2,0:T(2,128)} %copy.261), calls=%async_computation | async-start | bytes 262144 | tf_op jit(solution)/shard_map/all_to_all | solution.py:134
  19.6 43.1 %collective-permute-start.1 = (f32[5,8,1,128]{3,1,2,0:T(8,128)}, f32[5,8,1,128]{3,1,2,0:T(8,128)S(1)}, u32[]{:S(2)}, u32[]{:S(2)}) collective-permute-start(f32[5,8,1,128]{3,1,2,0:T(8,128)} %bitcast.176), channel_id=1, source_target_pairs={{8,0},{16,8},{24,16},{32,24},{40,32},{48,40},{56,48},{64,56},{72,6... | collective-permute-start | bytes 61448 | tf_op jit(solution)/shard_map/ppermute | solution.py:27
  25.0 37.7 %collective-permute-start = (f32[5,8,1,128]{3,1,2,0:T(8,128)}, f32[5,8,1,128]{3,1,2,0:T(8,128)S(1)}, u32[]{:S(2)}, u32[]{:S(2)}) collective-permute-start(f32[5,8,1,128]{3,1,2,0:T(8,128)} %bitcast.175), channel_id=1, source_target_pairs={{0,8},{8,16},{16,24},{24,32},{32,40},{40,48},{48,56},{56,64},{64,7... | collective-permute-start | bytes 61448 | tf_op jit(solution)/shard_map/ppermute | solution.py:25
  27.7 278.8 %collective-permute-start.5 = (f32[8,3,128]{2,0,1:T(8,128)}, f32[8,3,128]{2,0,1:T(8,128)}, u32[]{:S(2)}, u32[]{:S(2)}) collective-permute-start(f32[8,3,128]{2,0,1:T(8,128)} %convolution_bitcast_fusion.22), channel_id=1, source_target_pairs={{1,0},{2,1},{3,2},{4,3},{5,4},{6,5},{7,6},{8,7},{9,8},{10,9},{11,1... | collective-permute-start | bytes 36872 | tf_op jit(solution)/shard_map/ppermute | solution.py:27
  28.3 245.5 %collective-permute-start.4 = (f32[8,3,128]{2,1,0:T(4,128)S(1)}, f32[8,3,128]{2,1,0:T(4,128)S(1)}, u32[]{:S(2)}, u32[]{:S(2)}) collective-permute-start(f32[8,3,128]{2,1,0:T(4,128)S(1)} %copy.275), channel_id=1, source_target_pairs={{0,1},{1,2},{2,3},{3,4},{4,5},{5,6},{6,7},{7,8},{8,9},{9,10},{10,1... | collective-permute-start | bytes 36872 | tf_op jit(solution)/shard_map/ppermute | solution.py:25
  30.7 29.7 %copy-start.9 = (f32[5,1,128,128]{3,2,1,0:T(8,128)}, f32[5,1,128,128]{3,2,1,0:T(8,128)S(1)}, u32[]{:S(2)}) copy-start(f32[5,1,128,128]{3,2,1,0:T(8,128)S(1)} %get-tuple-element.230) | copy-start | bytes 983044
  30.7 206.2 %copy-start.28 = (s32[1024]{0:T(1024)}, s32[1024]{0:T(1024)S(1)}, u32[]{:S(2)}) copy-start(s32[1024]{0:T(1024)S(1)} %pad_clamp_fusion.2) | copy-start | bytes 12292
  45.0 65.5 %all-to-all-start.1 = ((f32[256,3,128]{2,1,0:T(4,128)}), f32[256,3,128]{2,1,0:T(4,128)}, u32[]{:S(2)}, u32[]{:S(2)}) async-start(f32[256,3,128]{2,1,0:T(4,128)} %scatter_fusion), calls=%async_computation.1 | async-start | bytes 1048576 | tf_op jit(solution)/shard_map/all_to_all | solution.py:133
  64.7 4.2 copy-start.5
  73.4 13.5 %collective-permute-start.2 = (f32[5,8,130,1]{2,1,3,0:T(8,128)S(1)}, f32[5,8,130,1]{2,1,3,0:T(8,128)}, u32[]{:S(2)}, u32[]{:S(2)}) collective-permute-start(f32[5,8,130,1]{2,1,3,0:T(8,128)S(1)} %copy.253), channel_id=1, source_target_pairs={{0,1},{1,2},{2,3},{3,4},{4,5},{5,6},{6,7},{7,0},{8,9},{9,10},{10,1... | collective-permute-start | bytes 62408 | tf_op jit(solution)/shard_map/ppermute | solution.py:25
  78.9 2.7 copy-start.6
  78.9 11.2 %collective-permute-start.3 = (f32[5,8,130,1]{2,1,3,0:T(8,128)}, f32[5,8,130,1]{2,1,3,0:T(8,128)}, u32[]{:S(2)}, u32[]{:S(2)}) collective-permute-start(f32[5,8,130,1]{2,1,3,0:T(8,128)} %copy.254), channel_id=1, source_target_pairs={{1,0},{2,1},{3,2},{4,3},{5,4},{6,5},{7,6},{0,7},{9,8},{10,9},{11,1... | collective-permute-start | bytes 62408 | tf_op jit(solution)/shard_map/ppermute | solution.py:27
  213.7 23.2 %all-to-all-start.2 = ((f32[256,3,128]{2,1,0:T(4,128)}), f32[256,3,128]{2,1,0:T(4,128)}, u32[]{:S(2)}, u32[]{:S(2)}) async-start(f32[256,3,128]{2,1,0:T(4,128)} %convolution_bitcast_fusion.3), calls=%async_computation.2 | async-start | bytes 1048576 | tf_op jit(solution)/shard_map/all_to_all | solution.py:140
  223.9 14.8 %copy-start.14 = (f32[128,3,128]{2,0,1:T(8,128)S(1)}, f32[128,3,128]{2,0,1:T(8,128)}, u32[]{:S(2)}) copy-start(f32[128,3,128]{2,0,1:T(8,128)} %param.42) | copy-start | bytes 589828
  224.0 15.1 %copy-start.10 = (f32[5,1,128,128]{3,2,1,0:T(8,128)S(1)}, f32[5,1,128,128]{3,2,1,0:T(8,128)}, u32[]{:S(2)}) copy-start(f32[5,1,128,128]{3,2,1,0:T(8,128)} %copy-done.9) | copy-start | bytes 983044
  244.9 2.2 slice-start
  245.3 2.7 copy-start.7
  245.3 3.0 slice-start.1
  264.3 22.6 %all-to-all-start.3 = ((f32[256,3,128]{2,1,0:T(4,128)}), f32[256,3,128]{2,1,0:T(4,128)S(1)}, u32[]{:S(2)}, u32[]{:S(2)}) async-start(f32[256,3,128]{2,1,0:T(4,128)} %scatter_fusion.1), calls=%async_computation.3 | async-start | bytes 1048576 | tf_op jit(solution)/shard_map/all_to_all | solution.py:140
  273.8 32.7 %copy-start.23 = (s32[256,2]{0,1:T(2,128)}, s32[256,2]{0,1:T(2,128)S(1)}, u32[]{:S(2)}) copy-start(s32[256,2]{0,1:T(2,128)S(1)} %eq.26) | copy-start | bytes 6148
  276.2 30.3 %copy-start.19 = (f32[8,128]{1,0:T(8,128)S(1)}, f32[8,128]{1,0:T(8,128)}, u32[]{:S(2)}) copy-start(f32[8,128]{1,0:T(8,128)} %param.48) | copy-start | bytes 12292
  276.2 30.3 %copy-start.22 = (f32[8,3,128]{2,0,1:T(8,128)S(1)}, f32[8,3,128]{2,0,1:T(8,128)}, u32[]{:S(2)}) copy-start(f32[8,3,128]{2,0,1:T(8,128)} %param.49) | copy-start | bytes 36868
  307.7 2.5 collective-permute-start.6
  310.2 3.1 collective-permute-start.7
  312.6 145.5 %copy-start.16 = (f32[8,8,3,128]{3,1,2,0:T(8,128)S(1)}, f32[8,8,3,128]{3,1,2,0:T(8,128)}, u32[]{:S(2)}) copy-start(f32[8,8,3,128]{3,1,2,0:T(8,128)} %param.51) | copy-start | bytes 294916
  312.6 227.6 %copy-start.17 = (f32[8,8,3,128]{3,1,2,0:T(8,128)S(1)}, f32[8,8,3,128]{3,1,2,0:T(8,128)}, u32[]{:S(2)}) copy-start(f32[8,8,3,128]{3,1,2,0:T(8,128)} %param.52) | copy-start | bytes 294916
  423.5 2.2 collective-permute-start.8
  424.9 3.3 collective-permute-start.9
  574.3 18.0 %all-to-all-start.4 = ((f32[256,3,128]{2,1,0:T(4,128)}), f32[256,3,128]{2,1,0:T(4,128)S(1)}, u32[]{:S(2)}, u32[]{:S(2)}) async-start(f32[256,3,128]{2,1,0:T(4,128)} %convolution_bitcast_fusion.2), calls=%async_computation.4 | async-start | bytes 1048576 | tf_op jit(solution)/shard_map/all_to_all | solution.py:140
  578.4 47.9 %collective-permute-start.10 = (f32[8,3,128]{2,0,1:T(8,128)S(1)}, f32[8,3,128]{2,0,1:T(8,128)S(1)}, u32[]{:S(2)}, u32[]{:S(2)}) collective-permute-start(f32[8,3,128]{2,0,1:T(8,128)S(1)} %bitcast_subtract_fusion.1), channel_id=1, source_target_pairs={{0,1},{1,2},{2,3},{3,4},{4,5},{5,6},{6,7},{7,8},{8,9},{9,10},{10,1... | collective-permute-start | bytes 36872 | tf_op jit(solution)/shard_map/ppermute | solution.py:25
  603.0 2.6 copy-start.15
  603.0 3.7 copy-start.27
  619.1 18.0 %all-to-all-start.5 = ((f32[256,3,128]{2,1,0:T(4,128)}), f32[256,3,128]{2,1,0:T(4,128)S(1)}, u32[]{:S(2)}, u32[]{:S(2)}) async-start(f32[256,3,128]{2,1,0:T(4,128)} %scatter_fusion.2), calls=%async_computation.5 | async-start | bytes 1048576 | tf_op jit(solution)/shard_map/all_to_all | solution.py:140
  624.9 31.9 %collective-permute-start.11 = (f32[8,3,128]{2,0,1:T(8,128)S(1)}, f32[8,3,128]{2,0,1:T(8,128)S(1)}, u32[]{:S(2)}, u32[]{:S(2)}) collective-permute-start(f32[8,3,128]{2,0,1:T(8,128)S(1)} %convolution_bitcast_fusion.18), channel_id=1, source_target_pairs={{1,0},{2,1},{3,2},{4,3},{5,4},{6,5},{7,6},{8,7},{9,8},{10,9},{11,1... | collective-permute-start | bytes 36872 | tf_op jit(solution)/shard_map/ppermute | solution.py:27
  628.7 28.1 %copy-start.24 = (s32[256,2]{0,1:T(2,128)S(1)}, s32[256,2]{0,1:T(2,128)}, u32[]{:S(2)}) copy-start(s32[256,2]{0,1:T(2,128)} %copy-done.23) | copy-start | bytes 6148
  657.2 2.5 collective-permute-start.12
  659.7 3.1 collective-permute-start.13
  662.2 145.3 %slice-start.2 = ((f32[8,8,3,128]{3,1,2,0:T(8,128)}), f32[7,8,3,128]{3,1,2,0:T(8,128)S(1)}, s32[]{:S(2)}) async-start(f32[8,8,3,128]{3,1,2,0:T(8,128)} %param.51), calls=%async_computation.8 | async-start | bytes 172032 | tf_op jit(solution)/shard_map/slice | solution.py:247
  720.5 169.1 %slice-start.3 = ((f32[8,8,3,128]{3,1,2,0:T(8,128)}), f32[7,8,3,128]{3,1,2,0:T(8,128)S(1)}, s32[]{:S(2)}) async-start(f32[8,8,3,128]{3,1,2,0:T(8,128)} %param.52), calls=%async_computation.9 | async-start | bytes 172032 | tf_op jit(solution)/shard_map/slice | solution.py:249
  772.8 2.3 collective-permute-start.14
  774.2 3.4 collective-permute-start.15
  835.2 55.2 %copy-start.21 = (f32[8,3,128]{2,0,1:T(8,128)}, f32[8,3,128]{2,0,1:T(8,128)S(1)}, u32[]{:S(2)}) copy-start(f32[8,3,128]{2,0,1:T(8,128)S(1)} %get-tuple-element.205) | copy-start | bytes 36868
  (7 other events, 11.3 us)
